TPU v7x, 256 devices: a whole 4x4x8 slice. The times are simulated.
256 devices in a mesh: seq: 128 (over x, z, y), head: 2 (over core).
Axes of the slice: x: 4, y: 4, z: 8, core: 2. Of those that a mesh axis runs over, the one named last changes fastest.
Arguments:
- queries: bfloat16 [16384, 512], P('seq', 'head')
- keys_values: bfloat16 [16384, 256], P(('seq', 'head'))
- selected: int32 [128, 3], replicated, may hold values from -1 to 31, as said below
Outputs:
- attended: bfloat16 [16384, 512], P('seq', 'head')
Inputs may be any that keep to these rules, and one draw needn't show every extreme that they name: selected[c, 0] = c // 4, the span's own block; selected[c, 1] and selected[c, 2] are two different blocks before it, chosen at random; where fewer than two earlier blocks exist, the missing entries are -1 (column 1 first filled).
All inputs are finite; a program needn't handle non-finite values.
Results may differ from a plain program's by a relative error of at most 0.0052.
Values may be sent and summed in bfloat16 or wider, within the bound.
A program may use at most 64 MiB of HBM per device.

v0:
```python
import jax
import jax.numpy as jnp
from jax import lax
from jax.sharding import PartitionSpec as P

DH = 128
GROUP = 4
TOPK = 3


def swapped(block, axis, stride):
    count = lax.axis_size(axis)
    route = []
    for low in range(count):
        high = low | 1 << stride
        if high != low and high < count:
            route += [(low, high), (high, low)]
    return lax.ppermute(block, axis, route)


def attend_rows(query_rows, block_kv, query_pos, key_pos):
    count = query_rows.shape[0]
    heads = query_rows.shape[1] // DH
    shaped = query_rows.reshape(count, heads, DH)
    keys = block_kv[:, :DH]
    values = block_kv[:, DH:]
    scores = jnp.einsum("nhd,kd->hnk", shaped, keys, preferred_element_type=jnp.float32) * DH ** (
        -0.5
    )
    if query_pos is not None:
        allowed = key_pos[None, :] <= query_pos[:, None]
        scores = jnp.where(allowed[None], scores, -1e30)
    top = jnp.max(scores, axis=-1)
    expo = jnp.exp(scores - top[..., None])
    total = jnp.sum(expo, axis=-1)
    weights = expo.astype(jnp.bfloat16)
    outputs = jnp.einsum("hnk,kd->nhd", weights, values, preferred_element_type=jnp.float32)
    outputs = outputs / jnp.transpose(total)[..., None]
    lse = jnp.transpose(top + jnp.log(total))
    return (outputs, lse)


def blocked_attend(query_rows, block_kv, query_pos, key_pos):
    count = query_rows.shape[0]
    step_rows = 512 if count % 512 == 0 else count
    steps = count // step_rows
    grouped = query_rows.reshape(steps, step_rows, query_rows.shape[1])
    if query_pos is None:
        outputs, lse = lax.map(lambda rows: attend_rows(rows, block_kv, None, None), grouped)
    else:
        grouped_pos = query_pos.reshape(steps, step_rows)
        outputs, lse = lax.map(
            lambda pair: attend_rows(pair[0], block_kv, pair[1], key_pos), (grouped, grouped_pos)
        )
    return (outputs.reshape(count, outputs.shape[2], DH), lse.reshape(count, lse.shape[2]))


def shards(queries, keys_values, selected):
    kv_rows = lax.all_gather(keys_values, "head", axis=0, tiled=True)
    tok_rows = kv_rows.shape[0]
    seq_count = lax.axis_size("seq")
    seq_index = lax.axis_index("seq")
    piece_rows = tok_rows // GROUP
    block_count = seq_count // GROUP
    width = queries.shape[1]
    heads = width // DH
    block_kv = kv_rows
    for bit_number in range(GROUP.bit_length() - 1):
        partner = swapped(block_kv, "seq", bit_number)
        upper = seq_index >> bit_number & 1 == 1
        block_kv = jnp.where(
            upper, jnp.concatenate([partner, block_kv], 0), jnp.concatenate([block_kv, partner], 0)
        )
    row_sel = lax.dynamic_slice_in_dim(selected, seq_index, 1, 0)[0]
    my_block = seq_index // GROUP
    block_start = my_block * GROUP * tok_rows
    query_pos = seq_index * tok_rows + jnp.arange(tok_rows, dtype=jnp.int32)
    key_pos = block_start + jnp.arange(GROUP * tok_rows, dtype=jnp.int32)
    pieces = queries.reshape(GROUP, piece_rows, width)
    tiled = jnp.tile(pieces, (block_count, 1, 1))
    target = jnp.arange(seq_count, dtype=jnp.int32) // GROUP
    wanted = (target == row_sel[1]) | (target == row_sel[2])
    outgoing = jnp.where(wanted[:, None, None], tiled, jnp.zeros_like(tiled))
    arrived = lax.all_to_all(outgoing, "seq", split_axis=0, concat_axis=0, tiled=True)
    senders = arrived.shape[0]
    items = arrived.shape[1]
    flat = arrived.reshape(senders * items, width)
    outputs, lse = blocked_attend(flat, block_kv, None, None)
    outputs = outputs.astype(jnp.bfloat16).reshape(senders, items, width)
    lse = lse.reshape(senders, items, heads)
    back_out = lax.all_to_all(outputs, "seq", split_axis=0, concat_axis=0, tiled=True)
    back_lse = lax.all_to_all(lse, "seq", split_axis=0, concat_axis=0, tiled=True)
    own_out, own_lse = blocked_attend(queries, block_kv, query_pos, key_pos)
    outs_list = [own_out]
    lse_list = [own_lse]
    for column in range(1, TOPK):
        block_id = row_sel[column]
        safe = jnp.maximum(block_id, 0) * GROUP
        part_out = (
            lax.dynamic_slice_in_dim(back_out, safe, GROUP, 0)
            .reshape(tok_rows, heads, DH)
            .astype(jnp.float32)
        )
        part_lse = lax.dynamic_slice_in_dim(back_lse, safe, GROUP, 0).reshape(tok_rows, heads)
        part_lse = jnp.where(block_id >= 0, part_lse, -1e30)
        outs_list.append(part_out)
        lse_list.append(part_lse)
    lse_all = jnp.stack(lse_list)
    outs_all = jnp.stack(outs_list)
    largest = jnp.max(lse_all, axis=0)
    factor = jnp.exp(lse_all - largest[None])
    merged = jnp.sum(factor[..., None] * outs_all, axis=0) / jnp.sum(factor, axis=0)[..., None]
    return merged.reshape(tok_rows, width).astype(jnp.bfloat16)


def solution(mesh):
    in_specs = (P("seq", "head"), P(("seq", "head"), None), P())
    out_specs = P("seq", "head")
    return jax.shard_map(shards, mesh=mesh, in_specs=in_specs, out_specs=out_specs, check_vma=False)
```

profile of v0, /device:TPU:1, one launch (start us, length us, event | category | flops | bytes accessed | tf_op | source)
XLA Modules:
  0.0 169.9 jit_solution(15113427760931273586)
XLA Ops:
  0.0 0.7 copy-done
  0.8 0.6 fusion.31
  1.4 1.3 compare_or_fusion
  2.6 2.4 %bitcast_select_fusion = bf16[128,32,256]{2,1,0:T(8,128)(2,1)} fusion(pred[128]{0:T(512)(128)(4,1)S(1)} %compare_or_fusion, bf16[4,32,256]{2,1,0:T(8,128)(2,1)} %bitcast.127), kind=kLoop, calls=%fused_computation.20 | loop fusion | flops 1048576 | bytes 2162816 | tf_op jit(solution)/shard_map/jit(_where)/select_n | solution.py:83
  5.0 16.5 %all-to-all-start = ((bf16[128,32,256]{2,1,0:T(8,128)(2,1)}), bf16[128,32,256]{2,1,0:T(8,128)(2,1)S(1)}, u32[]{:S(2)}, u32[]{:S(2)}) async-start(bf16[128,32,256]{2,1,0:T(8,128)(2,1)} %bitcast_select_fusion), calls=%async_computation | async-start | bytes 4194304 | tf_op jit(solution)/shard_map/all_to_all | solution.py:84
  21.4 2.5 %all_gather.3 = bf16[128,256]{1,0:T(8,128)(2,1)S(1)} all-gather(bf16[64,256]{1,0:T(8,128)(2,1)S(1)} %copy-done.2), channel_id=1, replica_groups=mesh['seq'=128,'head'=2] {'head'}, dimensions={0}, use_global_device_ids=true | all-gather | bytes 98304 | tf_op jit(solution)/shard_map/all_gather | solution.py:59
  23.9 0.9 collective-permute-start
  24.8 4.9 %collective-permute-done = bf16[128,256]{1,0:T(8,128)(2,1)S(1)} collective-permute-done((bf16[128,256]{1,0:T(8,128)(2,1)S(1)}, bf16[128,256]{1,0:T(8,128)(2,1)S(1)}, u32[]{:S(2)}, u32[]{:S(2)}) %collective-permute-start) | collective-permute-done | bytes 65568 | tf_op jit(solution)/shard_map/ppermute | solution.py:18
  29.7 3.1 %collective-permute-start.1 = (bf16[256,256]{1,0:T(8,128)(2,1)S(1)}, bf16[256,256]{1,0:T(8,128)(2,1)S(1)}, u32[]{:S(2)}, u32[]{:S(2)}) collective-permute-start(bf16[256,256]{1,0:T(8,128)(2,1)S(1)} %maximum_select_fusion.1), channel_id=1, source_target_pairs={{0,4},{4,0},{2,6},{6,2},{8,12},{12,8},{10,14},{14,10},{16,20},{20,... | collective-permute-start | bytes 393224 | tf_op jit(solution)/shard_map/ppermute | solution.py:18
  32.8 6.2 %collective-permute-done.1 = bf16[256,256]{1,0:T(8,128)(2,1)S(1)} collective-permute-done((bf16[256,256]{1,0:T(8,128)(2,1)S(1)}, bf16[256,256]{1,0:T(8,128)(2,1)S(1)}, u32[]{:S(2)}, u32[]{:S(2)}) %collective-permute-start.1) | collective-permute-done | bytes 131104 | tf_op jit(solution)/shard_map/ppermute | solution.py:18
  39.1 31.8 %all-to-all-done = bf16[128,32,256]{2,1,0:T(8,128)(2,1)S(1)} async-done(((bf16[128,32,256]{2,1,0:T(8,128)(2,1)}), bf16[128,32,256]{2,1,0:T(8,128)(2,1)S(1)}, u32[]{:S(2)}, u32[]{:S(2)}) %all-to-all-start) | async-done | bytes 2097184 | tf_op jit(solution)/shard_map/all_to_all | solution.py:84
  70.9 18.9 %while.2 = (s32[]{:T(128)}, bf16[8,512,2,128]{3,1,2,0:T(8,128)(2,1)}, f32[8,512,2]{1,0,2:T(8,128)S(1)}, bf16[8,512,256]{2,1,0:T(8,128)(2,1)S(1)}, bf16[512,256]{1,0:T(8,128)(2,1)S(1)}, /*index=5*/s32[]{:T(128)}, s32[]{:T(128)}) while((s32[]{:T(128)}, bf16[8,512,2,128]{3,1,2,0:T(8,128)(2,1)}, f32[8,512,2]{1,0,2:T(8,128)S(1)}, ...), condition=%wide.region_5.6_spmd, body=%wide.region_2.5_spmd.sunk | while | flops 272759808 | bytes 8437857 | solution.py:49
  71.9 1.3 fusion.45
  73.4 0.4 bitcast_reduce_fusion.2
  74.2 1.3 fusion.45
  76.6 1.3 fusion.45
  78.1 0.4 bitcast_reduce_fusion.2
  78.9 1.3 fusion.45
  81.3 1.3 fusion.45
  82.8 0.4 bitcast_reduce_fusion.2
  83.6 1.3 fusion.45
  86.0 1.3 fusion.45
  87.6 0.4 bitcast_reduce_fusion.2
  88.4 1.3 fusion.45
  89.8 0.8 copy.44
  90.6 9.6 %all-to-all-start.1 = ((f32[128,32,2]{1,2,0:T(2,128)}), f32[128,32,2]{1,2,0:T(2,128)S(1)}, u32[]{:S(2)}, u32[]{:S(2)}) async-start(f32[128,32,2]{1,2,0:T(2,128)} %copy.44), calls=%async_computation.1 | async-start | bytes 262144 | tf_op jit(solution)/shard_map/all_to_all | solution.py:92
  100.2 3.7 %copy.51 = bf16[8,512,2,128]{3,2,1,0:T(2,128)(2,1)S(1)} copy(bf16[8,512,2,128]{3,1,2,0:T(8,128)(2,1)} %get-tuple-element.55) | data formatting | bytes 4194304 | tf_op jit(solution)/shard_map/convert_element_type | solution.py:89
  104.0 2.6 %convert_element_type.48 = bf16[128,32,256]{2,1,0:T(8,128)(2,1)} reshape(bf16[8,512,2,128]{3,2,1,0:T(2,128)(2,1)S(1)} %copy.51) | data formatting | bytes 4194304 | tf_op jit(solution)/shard_map/convert_element_type | solution.py:89
  106.6 4.6 %all-to-all-done.1 = f32[128,32,2]{1,2,0:T(2,128)S(1)} async-done(((f32[128,32,2]{1,2,0:T(2,128)}), f32[128,32,2]{1,2,0:T(2,128)S(1)}, u32[]{:S(2)}, u32[]{:S(2)}) %all-to-all-start.1) | async-done | bytes 32800 | tf_op jit(solution)/shard_map/all_to_all | solution.py:92
  111.2 8.8 %all-to-all-start.2 = ((bf16[128,32,256]{2,1,0:T(8,128)(2,1)}), bf16[128,32,256]{2,1,0:T(8,128)(2,1)S(1)}, u32[]{:S(2)}, u32[]{:S(2)}) async-start(bf16[128,32,256]{2,1,0:T(8,128)(2,1)} %convert_element_type.48), calls=%async_computation.2 | async-start | bytes 4194304 | tf_op jit(solution)/shard_map/all_to_all | solution.py:91
  123.7 45.0 %all-to-all-done.2 = bf16[128,32,256]{2,1,0:T(8,128)(2,1)S(1)} async-done(((bf16[128,32,256]{2,1,0:T(8,128)(2,1)}), bf16[128,32,256]{2,1,0:T(8,128)(2,1)S(1)}, u32[]{:S(2)}, u32[]{:S(2)}) %all-to-all-start.2) | async-done | bytes 2097184 | tf_op jit(solution)/shard_map/all_to_all | solution.py:91
  169.2 0.7 copy.54
  (85 shorter events, 8.4 us)
Async XLA Ops:
  0.0 0.7 copy-start
  5.0 16.5 %copy-start.2 = (bf16[64,256]{1,0:T(8,128)(2,1)S(1)}, bf16[64,256]{1,0:T(8,128)(2,1)}, u32[]{:S(2)}) copy-start(bf16[64,256]{1,0:T(8,128)(2,1)} %param.6) | copy-start | bytes 98308
  5.0 65.9 %all-to-all-start = ((bf16[128,32,256]{2,1,0:T(8,128)(2,1)}), bf16[128,32,256]{2,1,0:T(8,128)(2,1)S(1)}, u32[]{:S(2)}, u32[]{:S(2)}) async-start(bf16[128,32,256]{2,1,0:T(8,128)(2,1)} %bitcast_select_fusion), calls=%async_computation | async-start | bytes 4194304 | tf_op jit(solution)/shard_map/all_to_all | solution.py:84
  23.9 5.8 %collective-permute-start = (bf16[128,256]{1,0:T(8,128)(2,1)S(1)}, bf16[128,256]{1,0:T(8,128)(2,1)S(1)}, u32[]{:S(2)}, u32[]{:S(2)}) collective-permute-start(bf16[128,256]{1,0:T(8,128)(2,1)S(1)} %all_gather.3), channel_id=1, source_target_pairs={{0,2},{2,0},{4,6},{6,4},{8,10},{10,8},{12,14},{14,12},{16,18},{18,... | collective-permute-start | bytes 196616 | tf_op jit(solution)/shard_map/ppermute | solution.py:18
  29.7 9.2 %collective-permute-start.1 = (bf16[256,256]{1,0:T(8,128)(2,1)S(1)}, bf16[256,256]{1,0:T(8,128)(2,1)S(1)}, u32[]{:S(2)}, u32[]{:S(2)}) collective-permute-start(bf16[256,256]{1,0:T(8,128)(2,1)S(1)} %maximum_select_fusion.1), channel_id=1, source_target_pairs={{0,4},{4,0},{2,6},{6,2},{8,12},{12,8},{10,14},{14,10},{16,20},{20,... | collective-permute-start | bytes 393224 | tf_op jit(solution)/shard_map/ppermute | solution.py:18
  90.6 20.6 %all-to-all-start.1 = ((f32[128,32,2]{1,2,0:T(2,128)}), f32[128,32,2]{1,2,0:T(2,128)S(1)}, u32[]{:S(2)}, u32[]{:S(2)}) async-start(f32[128,32,2]{1,2,0:T(2,128)} %copy.44), calls=%async_computation.1 | async-start | bytes 262144 | tf_op jit(solution)/shard_map/all_to_all | solution.py:92
  106.6 16.1 %copy-start.1 = (bf16[128,256]{1,0:T(8,128)(2,1)S(1)}, bf16[128,256]{1,0:T(8,128)(2,1)}, u32[]{:S(2)}) copy-start(bf16[128,256]{1,0:T(8,128)(2,1)} %param.5) | copy-start | bytes 196612
  111.2 57.5 %all-to-all-start.2 = ((bf16[128,32,256]{2,1,0:T(8,128)(2,1)}), bf16[128,32,256]{2,1,0:T(8,128)(2,1)S(1)}, u32[]{:S(2)}, u32[]{:S(2)}) async-start(bf16[128,32,256]{2,1,0:T(8,128)(2,1)} %convert_element_type.48), calls=%async_computation.2 | async-start | bytes 4194304 | tf_op jit(solution)/shard_map/all_to_all | solution.py:91
where the time goes:
time: 173 us; the launch traced here: 170 us
  waiting for transfers between devices  92.5 us (53%)
  starting transfers between devices  38.8 us (22%)
  matrix products  14.1 us (8%)
  local copies, waits for them, and re-layouts  11.9 us (7%)
  other arithmetic  7.06 us (4%)
  between operations  2.73 us (2%)
  blocking collectives  2.46 us (1%)
    all_to_all x1, waiting for transfers between devices, shards(): lax.all_to_all(outputs, 'seq', split_axis=0, concat_axis=0, tiled=True)  45 us
    all_to_all x1, waiting for transfers between devices, shards(): lax.all_to_all(outgoing, 'seq', split_axis=0, concat_axis=0, tiled=True)  31.8 us
    all_to_all x1, starting transfers between devices, shards(): lax.all_to_all(outgoing, 'seq', split_axis=0, concat_axis=0, tiled=True)  16.5 us
    ppermute x2, waiting for transfers between devices, swapped(): return lax.ppermute(block, axis, route)  11.1 us
    dot_general x9, matrix products, attend_rows(): jnp.einsum('hnk,kd->nhd', weights, values, preferred_element_type=jnp.flo...  10.4 us
    all_to_all x1, starting transfers between devices, shards(): lax.all_to_all(lse, 'seq', split_axis=0, concat_axis=0, tiled=True)  9.61 us
    all_to_all x1, starting transfers between devices, shards(): lax.all_to_all(outputs, 'seq', split_axis=0, concat_axis=0, tiled=True)  8.8 us
    convert_element_type x2, local copies, waits for them, and re-layouts, shards(): outputs = outputs.astype(jnp.bfloat16).reshape(senders, items, width)  6.37 us
  transfers between devices with their start and end apart: 5, of which 5 were waited for; matrix products, arithmetic and copies ran while one was open for 4% of the time, Pallas kernels for 0%

commit v1 on v0

v1 whole, which is shorter than its diff:
```python
import jax
import jax.numpy as jnp
from jax import lax
from jax.experimental import pallas as pl
from jax.experimental.pallas import tpu as pltpu
from jax.sharding import PartitionSpec as P

DH = 128
NX, NZ, NY = 4, 8, 4
ROWS = 64
HALF = ROWS // 2
MESH = pl.DeviceIdType.MESH
NEG = -1e30


def a_next(dx, dz):
    out = []
    if dz == 0:
        if dx == 0:
            out += [("x", 1, 1, 0), ("x", -1, 3, 0), ("x", 2, 2, 0)]
        out += [("z", 1, dx, 1), ("z", -1, dx, 7)]
    elif dz < 3 or (dz == 3 and dx % 2 == 0):
        out += [("z", 1, dx, dz + 1)]
    elif dz > 5 or (dz == 5 and dx % 2 == 1):
        out += [("z", -1, dx, dz - 1)]
    return out


def b_next(dx, dz):
    out = []
    if dx == 0:
        if dz == 0:
            out += [("z", 1, 0, 1), ("z", -1, 0, 7)]
        elif dz < 4:
            out += [("z", 1, 0, dz + 1)]
        elif dz > 5:
            out += [("z", -1, 0, dz - 1)]
        out += [("x", 1, 1, dz), ("x", -1, 3, dz)]
    elif dx == 1 and dz % 2 == 0:
        out += [("x", 1, 2, dz)]
    elif dx == 3 and dz % 2 == 1:
        out += [("x", -1, 2, dz)]
    return out


def levels(follow):
    cost = {(0, 0): 0}
    order = [(0, 0)]
    for node in order:
        for _, step, dx, dz in follow(*node):
            cost[(dx, dz)] = cost[node] + abs(step)
            order.append((dx, dz))
    return cost


def kernel(q_ref, kv_ref, sel_ref, o_ref, kvb, kvown, kvsel, stg, a_send, a_recv, b_send, b_recv, own_send, own_recv,
           y_send, y_recv, p_send, p_recv):
    s = lax.axis_index("seq")
    h = lax.axis_index("head")
    x = s // (NZ * NY)
    z = (s // NY) % NZ
    y = s % NY
    base = s - y

    def dev(axis, step):
        if axis == "x":
            return (((x + step + NX) % NX) * (NZ * NY) + z * NY + y, h)
        if axis == "z":
            return (x * (NZ * NY) + ((z + step + NZ) % NZ) * NY + y, h)
        return (base + (y + step) % NY, h)

    partner = (s, 1 - h)
    near = [dev("x", 1), dev("x", 2), dev("x", 3), dev("z", 1), dev("z", -1), partner]
    for k in range(1, NY):
        near += [dev("y", k), (dev("y", k)[0], 1 - h)]
    barrier = pltpu.get_barrier_semaphore()
    for d in near:
        pl.semaphore_signal(barrier, inc=1, device_id=d, device_id_type=MESH)
    pl.semaphore_wait(barrier, len(near))

    started = []

    def send(src, dst, ssem, rsem, d):
        c = pltpu.make_async_remote_copy(src_ref=src, dst_ref=dst, send_sem=ssem, recv_sem=rsem, device_id=d,
                                         device_id_type=MESH)
        c.start()
        started.append(c)
        return c

    copies = {}

    def spread(kind, node):
        follow = a_next if kind == "a" else b_next
        ssem, rsem = (a_send, a_recv) if kind == "a" else (b_send, b_recv)
        rows = pl.ds(0, HALF) if kind == "a" else pl.ds(HALF, HALF)
        src = kv_ref.at[rows] if node == (0, 0) else kvb.at[node[0] * NZ + node[1], rows]
        for axis, step, dx, dz in follow(*node):
            r = dx * NZ + dz
            copies[(kind, dx, dz)] = send(src, kvb.at[r, rows], ssem.at[r], rsem.at[r], dev(axis, step))

    spread("b", (0, 0))
    spread("a", (0, 0))
    slot = y * 2 + h
    own_rows = pl.ds(pl.multiple_of(slot * ROWS, ROWS), ROWS)
    owns = []
    for i, k in enumerate(range(1, NY)):
        for j, hh in enumerate((h, 1 - h)):
            owns.append(send(kv_ref, kvown.at[own_rows], own_send.at[i * 2 + j], own_recv.at[i * 2 + j],
                             (dev("y", k)[0], hh)))
    owns.append(send(kv_ref, kvown.at[own_rows], own_send.at[6], own_recv.at[6], partner))
    kvown[own_rows] = kv_ref[...]
    kvb[0] = kv_ref[...]

    q = jnp.concatenate([q_ref[:, :DH], q_ref[:, DH:]], axis=0)
    scale = DH ** -0.5

    def scores(keys):
        return lax.dot_general(q, keys, (((1,), (1,)), ((), ())), preferred_element_type=jnp.float32) * scale

    def fold(state, sc, values):
        top = jnp.max(sc, axis=1, keepdims=True)
        if state is not None:
            top = jnp.maximum(top, state[0])
        expo = jnp.exp(sc - top)
        total = jnp.sum(expo, axis=1, keepdims=True)
        acc = jnp.dot(expo.astype(jnp.bfloat16), values, preferred_element_type=jnp.float32)
        if state is not None:
            factor = jnp.exp(state[0] - top)
            total = total + state[1] * factor
            acc = acc + state[2] * factor
        return (top, total, acc)

    cost_a, cost_b = levels(a_next), levels(b_next)
    todo = [(c, 0, "a", n) for n, c in cost_a.items() if c] + [(c, 1, "b", n) for n, c in cost_b.items() if c]
    todo.sort(key=lambda t: (t[0], t[1]))
    state = None
    for cost, _, kind, node in todo:
        if cost == 4 and state is None:
            for c in owns:
                c.wait_recv()
            sc = scores(kvown[:, :DH])
            row = lax.broadcasted_iota(jnp.int32, sc.shape, 0) % (2 * ROWS) + y * (2 * ROWS)
            col = lax.broadcasted_iota(jnp.int32, sc.shape, 1)
            state = fold(None, jnp.where(col <= row, sc, NEG), kvown[:, DH:])
        copies[(kind,) + node].wait_recv()
        spread(kind, node)

    my_rows = pl.ds(pl.multiple_of(h * ROWS, ROWS), ROWS)

    def rel(block):
        block = jnp.maximum(block, 0)
        bx = block // NZ
        bz = block % NZ
        return ((x - bx + NX) % NX) * NZ + (z - bz + NZ) % NZ

    for k in (2, 1, 3, 0):
        span = base + (y + k) % NY
        for j in range(2):
            part = kvb[rel(sel_ref[span, j + 1])]
            if k:
                stg[k - 1, j] = part
            else:
                kvsel[0, j, my_rows] = part
    ys = {}
    for k in (2, 1, 3):
        ys[k] = send(stg.at[k - 1], kvsel.at[k, :, my_rows], y_send.at[k], y_recv.at[k], dev("y", k))
    ps = {0: send(kvsel.at[0, :, my_rows], kvsel.at[0, :, my_rows], p_send.at[0], p_recv.at[0], partner)}

    valid = [sel_ref[s, j + 1] >= 0 for j in range(2)]
    for k in (1, 3, 2):
        ys[k].wait_recv()
        ps[k] = send(kvsel.at[k, :, my_rows], kvsel.at[k, :, my_rows], p_send.at[k], p_recv.at[k], partner)
    for k in (0, 1, 3, 2):
        ps[k].wait_recv()
        kv = kvsel[k].reshape(4 * ROWS, 2 * DH)
        sc = scores(kv[:, :DH])
        col = lax.broadcasted_iota(jnp.int32, sc.shape, 1)
        ok = jnp.where(col < 2 * ROWS, valid[0].astype(jnp.int32), valid[1].astype(jnp.int32))
        state = fold(state, jnp.where(ok > 0, sc, NEG), kv[:, DH:])

    out = state[2] / state[1]
    o_ref[:, :DH] = out[:2 * ROWS].astype(jnp.bfloat16)
    o_ref[:, DH:] = out[2 * ROWS:].astype(jnp.bfloat16)
    for c in started:
        c.wait_send()


def shards(queries, keys_values, selected):
    dma = pltpu.SemaphoreType.DMA
    return pl.pallas_call(
        kernel,
        out_shape=jax.ShapeDtypeStruct(queries.shape, jnp.bfloat16),
        in_specs=[pl.BlockSpec(memory_space=pltpu.VMEM)] * 2 + [pl.BlockSpec(memory_space=pltpu.SMEM)],
        out_specs=pl.BlockSpec(memory_space=pltpu.VMEM),
        scratch_shapes=[
            pltpu.VMEM((NX * NZ, ROWS, 2 * DH), jnp.bfloat16),
            pltpu.VMEM((8 * ROWS, 2 * DH), jnp.bfloat16),
            pltpu.VMEM((NY, 2, 2 * ROWS, 2 * DH), jnp.bfloat16),
            pltpu.VMEM((NY - 1, 2, ROWS, 2 * DH), jnp.bfloat16),
            dma((NX * NZ,)), dma((NX * NZ,)), dma((NX * NZ,)), dma((NX * NZ,)),
            dma((7,)), dma((7,)), dma((NY,)), dma((NY,)), dma((NY,)), dma((NY,)),
        ],
        compiler_params=pltpu.CompilerParams(collective_id=0, has_side_effects=True),
    )(queries, keys_values, selected)


def solution(mesh):
    in_specs = (P("seq", "head"), P(("seq", "head"), None), P())
    out_specs = P("seq", "head")
    return jax.shard_map(shards, mesh=mesh, in_specs=in_specs, out_specs=out_specs, check_vma=False)
```

time: 173 us -> 43.4 us (0.25); the launches traced: 170 us -> 43.2 us
  waiting for transfers between devices: 92.5 us -> 0 us
  Pallas kernels: 0 us -> 40.3 us
  starting transfers between devices: 38.8 us -> 0 us
  matrix products: 14.1 us -> 0 us
  local copies, waits for them, and re-layouts: 11.9 us -> 2.89 us
  other arithmetic: 7.06 us -> 0 us
  between operations: 2.73 us -> 0.01 us
  blocking collectives: 2.46 us -> 0 us
    all_to_all x3 -> x0, waiting for transfers between devices: 81.4 us -> none  [the longest x1 45 us: shards(): lax.all_to_all(outputs, 'seq', split_axis=0, concat_axis=0, tiled=True)]
    pallas_call x0 -> x1, Pallas kernels: none -> 40.3 us  [shards(): pl.pallas_call(kernel, out_shape=jax.ShapeDtypeStruct(queries.shape, jnp....]
    all_to_all x3 -> x0, starting transfers between devices: 34.9 us -> none  [the longest x1 16.5 us: shards(): lax.all_to_all(outgoing, 'seq', split_axis=0, concat_axis=0, tiled=True)]
    dot_general x18 -> x0, matrix products: 14.1 us -> none  [the longest x9 10.4 us: attend_rows(): jnp.einsum('hnk,kd->nhd', weights, values, preferred_element_type=jnp.flo...]
    ppermute x2 -> x0, waiting for transfers between devices: 11.1 us -> none  [swapped(): return lax.ppermute(block, axis, route)]
    convert_element_type x7 -> x0, local copies, waits for them, and re-layouts: 7.44 us -> none  [the longest x2 6.37 us: shards(): outputs = outputs.astype(jnp.bfloat16).reshape(senders, items, width)]
    ppermute x2 -> x0, starting transfers between devices: 3.91 us -> none  [swapped(): return lax.ppermute(block, axis, route)]
    reduce_sum x11 -> x0, other arithmetic: 3.05 us -> none  [the longest x9 3 us: attend_rows(): total = jnp.sum(expo, axis=-1)]
  transfers between devices with their start and end apart: 5 -> 0, of which waited for: 5 -> 0; matrix products, arithmetic and copies ran while one was open for 4% -> 0% of each run, Pallas kernels for 0% -> 0%
where the time goes in v1:
time: 43.4 us; the launch traced here: 43.2 us
  Pallas kernels  40.3 us (93%)
  local copies, waits for them, and re-layouts  2.89 us (7%)
    pallas_call x1, Pallas kernels, shards(): pl.pallas_call(kernel, out_shape=jax.ShapeDtypeStruct(queries.shape, jnp....  40.3 us
    unnamed x2, local copies, waits for them, and re-layouts  2.89 us

profile of v1, /device:TPU:1, one launch (start us, length us, event | category | flops | bytes accessed | tf_op | source)
XLA Modules:
  0.0 43.2 jit_solution(17374438310421201245)
XLA Ops:
  0.0 1.4 %copy.4.sel_ref = s32[128,3]{1,0:T(8,128)} copy(s32[128,3]{0,1:T(4,128)} %param.5) | data formatting | bytes 3072 | tf_op args[2]
  1.4 40.3 %shard_map.37 = bf16[128,256]{1,0:T(8,128)(2,1)} custom-call(bf16[128,256]{1,0:T(8,128)(2,1)} %q_ref.1, bf16[64,256]{1,0:T(8,128)(2,1)} %kv_ref.1, s32[128,3]{1,0:T(8,128)} %copy.4.sel_ref), custom_call_target="tpu_custom_call" | custom-call | tf_op jit(solution)/shard_map/pallas_call | solution.py:190
  41.7 1.5 %copy.6 = bf16[128,256]{1,0:T(8,128)(2,1)} copy(bf16[128,256]{1,0:T(8,128)(2,1)} %shard_map.37) | data formatting | bytes 131072

commit v2 on v1

v2 whole, which is shorter than its diff:
```python
import jax
import jax.numpy as jnp
from jax import lax
from jax.experimental import pallas as pl
from jax.experimental.pallas import tpu as pltpu
from jax.sharding import PartitionSpec as P

DH = 128
NX, NZ, NY = 4, 8, 4
ROWS = 64
PART = ROWS // NX
MESH = pl.DeviceIdType.MESH
NEG = -1e30


def hops(step, size):
    return min(step % size, -step % size)


def kernel(q_hbm, kv_hbm, sel_hbm, o_ref, q_ref, kv_ref, sel_ref, kvb, kvown, kvsel, stg, in_sem, a_send, a_recv,
           own_send, own_recv, b_send, b_recv, p_send, p_recv):
    s = lax.axis_index("seq")
    h = lax.axis_index("head")
    x = s // (NZ * NY)
    z = (s // NY) % NZ
    y = s % NY

    loads = [pltpu.make_async_copy(a, b, in_sem.at[i])
             for i, (a, b) in enumerate(((kv_hbm, kv_ref), (sel_hbm, sel_ref), (q_hbm, q_ref)))]
    for c in loads:
        c.start()

    def seq_of(ax, az, ay):
        return (x + ax) % NX * (NZ * NY) + (z + az) % NZ * NY + (y + ay) % NY

    plane = [(ax, az) for ax in range(NX) for az in range(NZ) if (ax, az) != (0, 0)]
    plane.sort(key=lambda t: -(hops(t[0], NX) + hops(t[1], NZ)))
    group = [(ax, ay) for ax in range(NX) for ay in range(NY)]
    group.sort(key=lambda t: hops(t[0], NX) + hops(t[1], NY))
    partner = (s, 1 - h)

    near = [(seq_of(ax, az, 0), h) for ax, az in plane]
    near += [(seq_of(ax, 0, ay), h) for ax, ay in group if ay]
    near += [(seq_of(0, 0, ay), 1 - h) for ay in range(1, NY)] + [partner]
    barrier = pltpu.get_barrier_semaphore()
    for d in near:
        pl.semaphore_signal(barrier, inc=1, device_id=d, device_id_type=MESH)
    loads[0].wait()
    pl.semaphore_wait(barrier, len(near))

    started = []

    def send(src, dst, ssem, rsem, d):
        c = pltpu.make_async_remote_copy(src_ref=src, dst_ref=dst, send_sem=ssem, recv_sem=rsem, device_id=d,
                                         device_id_type=MESH)
        c.start()
        started.append(c)
        return c

    firsts = []
    for ax, az in plane:
        r = ax * NZ + az
        rows = pl.ds(pl.multiple_of((x + ax) % NX * PART, PART), PART)
        firsts.append(send(kv_ref.at[rows], kvb.at[r], a_send.at[r], a_recv.at[r], (seq_of(ax, az, 0), h)))
    slot = y * 2 + h
    own_rows = pl.ds(pl.multiple_of(slot * ROWS, ROWS), ROWS)
    owns = []
    for ay in range(NY):
        for j, hh in enumerate((h, 1 - h)):
            if ay or j:
                i = ay * 2 + j
                owns.append(send(kv_ref, kvown.at[own_rows], own_send.at[i], own_recv.at[i], (seq_of(0, 0, ay), hh)))
    kvown[own_rows] = kv_ref[...]
    kvb[0] = kv_ref[pl.ds(pl.multiple_of(x * PART, PART), PART)]

    loads[1].wait()
    loads[2].wait()

    def rel(block):
        block = jnp.maximum(block, 0)
        return (x - block // NZ + NX) % NX * NZ + (z - block % NZ + NZ) % NZ

    picks = []
    for ax, ay in group:
        span = seq_of(ax, 0, ay)
        picks.append([rel(sel_ref[j + 1, span]) for j in range(2)])
    valid = [sel_ref[j + 1, s] for j in range(2)]

    q = jnp.concatenate([q_ref[:, :DH], q_ref[:, DH:]], axis=0)
    scale = DH ** -0.5

    def scores(keys):
        return lax.dot_general(q, keys, (((1,), (1,)), ((), ())), preferred_element_type=jnp.float32) * scale

    def fold(state, sc, values):
        top = jnp.max(sc, axis=1, keepdims=True)
        if state is not None:
            top = jnp.maximum(top, state[0])
        expo = jnp.exp(sc - top)
        total = jnp.sum(expo, axis=1, keepdims=True)
        acc = jnp.dot(expo.astype(jnp.bfloat16), values, preferred_element_type=jnp.float32)
        if state is not None:
            factor = jnp.exp(state[0] - top)
            total = total + state[1] * factor
            acc = acc + state[2] * factor
        return (top, total, acc)

    for c in owns:
        c.wait_recv()
    sc = scores(kvown[:, :DH])
    row = lax.broadcasted_iota(jnp.int32, sc.shape, 0) % (2 * ROWS) + y * (2 * ROWS)
    col = lax.broadcasted_iota(jnp.int32, sc.shape, 1)
    state = fold(None, jnp.where(col <= row, sc, NEG), kvown[:, DH:])

    for c in firsts[::-1]:
        c.wait_recv()

    count = len(group)
    for i in range(count - 1, -1, -1):
        for j in range(2):
            part = kvb[picks[i][j]]
            if i:
                stg[i, j] = part
            else:
                kvsel[j, 0, h] = part
    seconds = {}
    for i in range(count - 1, 0, -1):
        ax, ay = group[i]
        seconds[i] = send(stg.at[i], kvsel.at[:, i, h], b_send.at[i], b_recv.at[i], (seq_of(ax, 0, ay), h))
    thirds = {}
    for i in range(count):
        if i:
            seconds[i].wait_recv()
        thirds[i] = send(kvsel.at[:, i, h], kvsel.at[:, i, h], p_send.at[i], p_recv.at[i], partner)

    lot = count // 2
    for half in range(2):
        for i in range(half * lot, half * lot + lot):
            thirds[i].wait_recv()
        kv = kvsel[:, half * lot:half * lot + lot].reshape(2 * lot * 2 * PART, 2 * DH)
        sc = scores(kv[:, :DH])
        col = lax.broadcasted_iota(jnp.int32, sc.shape, 1)
        ok = jnp.where(col < lot * 2 * PART, valid[0], valid[1])
        state = fold(state, jnp.where(ok >= 0, sc, NEG), kv[:, DH:])

    out = state[2] / state[1]
    o_ref[:, :DH] = out[:2 * ROWS].astype(jnp.bfloat16)
    o_ref[:, DH:] = out[2 * ROWS:].astype(jnp.bfloat16)
    for c in started:
        c.wait_send()


def shards(queries, keys_values, selected):
    dma = pltpu.SemaphoreType.DMA
    count = NX * NY
    return pl.pallas_call(
        kernel,
        out_shape=jax.ShapeDtypeStruct(queries.shape, jnp.bfloat16),
        in_specs=[pl.BlockSpec(memory_space=pl.ANY)] * 3,
        out_specs=pl.BlockSpec(memory_space=pltpu.VMEM),
        scratch_shapes=[
            pltpu.VMEM(queries.shape, jnp.bfloat16),
            pltpu.VMEM(keys_values.shape, jnp.bfloat16),
            pltpu.SMEM((3, NX * NZ * NY), jnp.int32),
            pltpu.VMEM((NX * NZ, PART, 2 * DH), jnp.bfloat16),
            pltpu.VMEM((8 * ROWS, 2 * DH), jnp.bfloat16),
            pltpu.VMEM((2, count, 2, PART, 2 * DH), jnp.bfloat16),
            pltpu.VMEM((count, 2, PART, 2 * DH), jnp.bfloat16),
            dma((3,)), dma((NX * NZ,)), dma((NX * NZ,)), dma((8,)), dma((8,)), dma((count,)), dma((count,)),
            dma((count,)), dma((count,)),
        ],
        compiler_params=pltpu.CompilerParams(collective_id=0, has_side_effects=True),
    )(queries, keys_values, selected.T)


def solution(mesh):
    in_specs = (P("seq", "head"), P(("seq", "head"), None), P())
    out_specs = P("seq", "head")
    return jax.shard_map(shards, mesh=mesh, in_specs=in_specs, out_specs=out_specs, check_vma=False)
```

time: 43.4 us -> 30.9 us (0.71)
  Pallas kernels: 40.3 us -> 29.2 us
  local copies, waits for them, and re-layouts: 2.89 us -> 1.47 us
    pallas_call x1, Pallas kernels: 40.3 us -> 29.2 us  [shards(): pl.pallas_call(kernel, out_shape=jax.ShapeDtypeStruct(queries.shape, jnp....]
    unnamed x2 -> x1, local copies, waits for them, and re-layouts: 2.89 us -> 1.47 us
where the time goes in v2:
time: 30.9 us; the launch traced here: 30.7 us
  Pallas kernels  29.2 us (94%)
  local copies, waits for them, and re-layouts  1.47 us (5%)
    pallas_call x1, Pallas kernels, shards(): pl.pallas_call(kernel, out_shape=jax.ShapeDtypeStruct(queries.shape, jnp....  29.2 us
    unnamed x1, local copies, waits for them, and re-layouts  1.47 us

profile of v2, /device:TPU:1, one launch (start us, length us, event | category | flops | bytes accessed | tf_op | source)
XLA Modules:
  0.0 30.7 jit_solution(15662261893929561871)
XLA Ops:
  0.0 29.2 %shard_map.37 = bf16[128,256]{1,0:T(8,128)(2,1)} custom-call(bf16[128,256]{1,0:T(8,128)(2,1)} %q_hbm.1, bf16[64,256]{1,0:T(8,128)(2,1)} %kv_hbm.1, s32[3,128]{1,0:T(4,128)} %bitcast.1), custom_call_target="tpu_custom_call" | custom-call | tf_op jit(solution)/shard_map/pallas_call | solution.py:156
  29.2 1.5 %copy.5 = bf16[128,256]{1,0:T(8,128)(2,1)} copy(bf16[128,256]{1,0:T(8,128)(2,1)} %shard_map.37) | data formatting | bytes 131072
